TPU v7x, 256 devices: a whole 4x4x8 slice. The times are simulated.
256 devices in a mesh: rep: 16 (over x, z_lo, core), fsdp: 16 (over y, z_hi).
Axes of the slice: x: 4, y: 4, z: 8 (z_hi: 4, z_lo: 2; z = z_hi * 2 + z_lo), core: 2. Of those that a mesh axis runs over, the one named last changes fastest.
Arguments:
- grad_gate: float32 [16, 128, 28672], P('rep', None, 'fsdp'), may hold values from -50 to 50
- grad_down: float32 [16, 256, 8192], P('rep', None, 'fsdp'), may hold values from -50 to 50
- param_gate: float32 [128, 28672], P(None, 'fsdp'), may hold values from -6 to 6
- mom1_gate: float32 [128, 28672], P(None, 'fsdp'), may hold values from -3 to 3
- mom2_gate: float32 [128, 28672], P(None, 'fsdp'), may hold values from 0.1 to 1
- param_down: float32 [256, 8192], P(None, 'fsdp'), may hold values from -6 to 6
- mom1_down: float32 [256, 8192], P(None, 'fsdp'), may hold values from -3 to 3
- mom2_down: float32 [256, 8192], P(None, 'fsdp'), may hold values from 0.1 to 1
Outputs:
- combined_gate: float32 [128, 28672], P(None, 'fsdp')
- new_param_gate: float32 [128, 28672], P(None, 'fsdp')
- new_mom1_gate: float32 [128, 28672], P(None, 'fsdp')
- new_mom2_gate: float32 [128, 28672], P(None, 'fsdp')
- combined_down: float32 [256, 8192], P(None, 'fsdp')
- new_param_down: float32 [256, 8192], P(None, 'fsdp')
- new_mom1_down: float32 [256, 8192], P(None, 'fsdp')
- new_mom2_down: float32 [256, 8192], P(None, 'fsdp')
All inputs are finite; a program needn't handle non-finite values.
Results may differ from a plain program's by a relative error of at most 0.0001.
Values sent between devices are 32-bit elements; how exact they have to be, the bound alone decides.
A program may use at most 64 MiB of HBM per device.

v0:
```python
import jax
import jax.numpy as jnp
from jax import lax
from jax.sharding import PartitionSpec as P


def swapped(x, axis, bit):
    return lax.ppermute(x, axis, [(i, i ^ 1 << bit) for i in range(lax.axis_size(axis))])


def adamw_rows(gradient, weights, moment_one, moment_two):
    new_one = 0.9 * moment_one + 0.1 * gradient
    new_two = 0.95 * moment_two + 0.05 * gradient * gradient
    corrected_one = new_one / (1.0 - 0.9**10)
    corrected_two = new_two / (1.0 - 0.95**10)
    step_size = corrected_one / (jnp.sqrt(corrected_two) + 1e-08) + 0.1 * weights
    return (weights - 0.05 * step_size, new_one, new_two)


def flip_sides(partials):
    return jnp.stack([partials[:, 0], partials[:, 2], partials[:, 1]], axis=1)


def group_sums(partials, level_bit, levels):
    running = lax.psum(partials, "fsdp")
    for upper_bit in range(level_bit, levels):
        received = swapped(running, "rep", upper_bit)
        if upper_bit == level_bit:
            received = flip_sides(received)
        running = running + received
    return running


def local(grad_gate, grad_down, param_gate, mom1_gate, mom2_gate, param_down, mom1_down, mom2_down):
    replicas = lax.axis_size("rep")
    levels = replicas.bit_length() - 1
    rep_index = lax.axis_index("rep")
    holdings = (grad_gate[0], grad_down[0])
    for step_level in range(levels):
        level_bit = levels - 1 - step_level
        upper_half = rep_index // (1 << level_bit) % 2
        retained = []
        outgoing = []
        for tensor in holdings:
            half_rows = tensor.shape[0] // 2
            retained.append(lax.dynamic_slice_in_dim(tensor, upper_half * half_rows, half_rows, 0))
            outgoing.append(
                lax.dynamic_slice_in_dim(tensor, (1 - upper_half) * half_rows, half_rows, 0)
            )
        incoming = swapped((outgoing[0], outgoing[1]), "rep", level_bit)
        rows_list = []
        for mine_part, their_part in zip(retained, incoming):
            rows_list.append(
                jnp.stack(
                    [
                        jnp.sum(mine_part * their_part),
                        jnp.sum(mine_part * mine_part),
                        jnp.sum(their_part * their_part),
                    ]
                )
            )
        partials = jnp.stack(rows_list)
        totals = group_sums(partials, level_bit, levels)
        merged = []
        for number in range(2):
            own_coef = 1.0 - totals[number, 0] / (2.0 * totals[number, 1])
            their_coef = 1.0 - totals[number, 0] / (2.0 * totals[number, 2])
            merged.append(own_coef * retained[number] + their_coef * incoming[number])
        holdings = (merged[0], merged[1])
    full_gate, full_down = (
        lax.all_gather(holdings[0], "rep", axis=0, tiled=True),
        lax.all_gather(holdings[1], "rep", axis=0, tiled=True),
    )
    gate_param, gate_one, gate_two = adamw_rows(full_gate, param_gate, mom1_gate, mom2_gate)
    down_param, down_one, down_two = adamw_rows(full_down, param_down, mom1_down, mom2_down)
    return (full_gate, gate_param, gate_one, gate_two, full_down, down_param, down_one, down_two)


def solution(mesh):
    in_specs = (
        P("rep", None, "fsdp"),
        P("rep", None, "fsdp"),
        P(None, "fsdp"),
        P(None, "fsdp"),
        P(None, "fsdp"),
        P(None, "fsdp"),
        P(None, "fsdp"),
        P(None, "fsdp"),
    )
    out_specs = (
        P(None, "fsdp"),
        P(None, "fsdp"),
        P(None, "fsdp"),
        P(None, "fsdp"),
        P(None, "fsdp"),
        P(None, "fsdp"),
        P(None, "fsdp"),
        P(None, "fsdp"),
    )
    return jax.shard_map(local, mesh=mesh, in_specs=in_specs, out_specs=out_specs, check_vma=False)
```

profile of v0, /device:TPU:1, one launch (start us, length us, event | category | flops | bytes accessed | tf_op | source)
XLA Modules:
  0.0 335.4 jit_solution(10442617677239891884)
XLA Ops:
  0.7 1.2 dynamic-slice_bitcast_fusion
  1.8 3.7 %collective-permute-start = (f32[64,1792]{1,0:T(8,128)S(1)}, f32[64,1792]{1,0:T(8,128)S(1)}, u32[]{:S(2)}, u32[]{:S(2)}) collective-permute-start(f32[64,1792]{1,0:T(8,128)S(1)} %dynamic-slice_bitcast_fusion), channel_id=1, source_target_pairs={{0,128},{16,144},{32,160},{48,176},{64,192},{80,208},{96,224},{112... | collective-permute-start | bytes 1376264 | tf_op jit(solution)/shard_map/ppermute | solution.py:8
  5.8 14.6 %collective-permute-done.1 = f32[128,512]{1,0:T(8,128)S(1)} collective-permute-done((f32[128,512]{1,0:T(8,128)S(1)}, f32[128,512]{1,0:T(8,128)S(1)}, u32[]{:S(2)}, u32[]{:S(2)}) %collective-permute-start.1) | collective-permute-done | bytes 262176 | tf_op jit(solution)/shard_map/ppermute | solution.py:8
  20.3 0.7 fusion.5
  21.0 0.7 fusion.2
  21.8 4.0 %maximum_bitcast_fusion = (f32[1,3]{1,0:T(1,128)S(1)}, f32[1,3]{1,0:T(1,128)S(1)}) fusion(f32[1]{0:T(128)} %bitcast.4, f32[1]{0:T(128)} %bitcast.3, f32[1]{0:T(128)} %bitcast.2, f32[1]{0:T(128)} %bitcast.10, f32[1]{0:T(128)} %bitcast.9, f32[1]{0:T(128)} %bitcast.8), kind=kLoop, calls=%fused_computation.62 | loop fusion | flops 12 | bytes 48 | tf_op jit(solution)/shard_map/stack | solution.py:62
  25.7 41.8 %psum.28 = f32[2,3]{1,0:T(2,128)S(1)} all-reduce(f32[2,3]{1,0:T(2,128)S(1)} %pad_maximum_fusion), channel_id=1, replica_groups=mesh['rep'=16,'fsdp'=16] {'fsdp'}, use_global_device_ids=true, to_apply=%region_6.7 | all-reduce | flops 6 | bytes 48 | tf_op jit(solution)/shard_map/psum | solution.py:25
  67.5 2.8 collective-permute-start.2
  70.4 1.2 collective-permute-done.2
  77.6 1.3 collective-permute-start.4
  79.3 2.2 collective-permute-done.4
  82.1 2.0 maximum_bitcast_fusion.3
  84.8 2.0 maximum_bitcast_fusion.2
  86.9 32.1 %psum.29 = f32[2,3]{1,0:T(2,128)S(1)} all-reduce(f32[2,3]{1,0:T(2,128)S(1)} %pad_maximum_fusion.1), channel_id=1, replica_groups=mesh['rep'=16,'fsdp'=16] {'fsdp'}, use_global_device_ids=true, to_apply=%region_13.14 | all-reduce | flops 6 | bytes 48 | tf_op jit(solution)/shard_map/psum | solution.py:25
  119.0 1.3 collective-permute-start.5
  120.3 1.5 collective-permute-done.5
  121.9 2.8 collective-permute-start.6
  124.7 1.4 collective-permute-done.6
  132.1 0.8 collective-permute-start.8
  132.9 0.8 collective-permute-start.7
  133.8 1.8 collective-permute-done.8
  136.2 2.0 maximum_bitcast_fusion.5
  138.9 2.0 maximum_bitcast_fusion.4
  140.9 33.9 %psum.30 = f32[2,3]{1,0:T(2,128)S(1)} all-reduce(f32[2,3]{1,0:T(2,128)S(1)} %pad_maximum_fusion.2), channel_id=1, replica_groups=mesh['rep'=16,'fsdp'=16] {'fsdp'}, use_global_device_ids=true, to_apply=%region_20.21 | all-reduce | flops 6 | bytes 48 | tf_op jit(solution)/shard_map/psum | solution.py:25
  174.8 0.9 collective-permute-start.9
  175.6 1.9 collective-permute-done.9
  177.7 1.2 collective-permute-start.10
  178.9 1.5 collective-permute-done.10
  180.5 2.7 collective-permute-start.11
  183.3 1.2 collective-permute-done.11
  190.3 31.6 %collective-permute-start.13 = (f32[16,512]{1,0:T(8,128)S(1)}, f32[16,512]{1,0:T(8,128)S(1)}, u32[]{:S(2)}, u32[]{:S(2)}) collective-permute-start(f32[16,512]{1,0:T(8,128)S(1)} %constant_dynamic-slice_fusion), channel_id=1, source_target_pairs={{0,16},{16,0},{32,48},{48,32},{64,80},{80,64},{96,112},{112,96},{1... | collective-permute-start | bytes 98312 | tf_op jit(solution)/shard_map/ppermute | solution.py:8
  222.1 0.7 collective-permute-done.13
  223.4 2.0 maximum_bitcast_fusion.7
  226.1 2.0 maximum_bitcast_fusion.6
  228.1 32.2 %psum.31 = f32[2,3]{1,0:T(2,128)S(1)} all-reduce(f32[2,3]{1,0:T(2,128)S(1)} %pad_maximum_fusion.3), channel_id=1, replica_groups=mesh['rep'=16,'fsdp'=16] {'fsdp'}, use_global_device_ids=true, to_apply=%region_27.28 | all-reduce | flops 6 | bytes 48 | tf_op jit(solution)/shard_map/psum | solution.py:25
  260.3 7.3 %collective-permute-start.14 = (f32[2,3]{1,0:T(2,128)S(1)}, f32[2,3]{1,0:T(2,128)S(1)}, u32[]{:S(2)}, u32[]{:S(2)}) collective-permute-start(f32[2,3]{1,0:T(2,128)S(1)} %psum.31), channel_id=1, source_target_pairs={{0,16},{16,0},{32,48},{48,32},{64,80},{80,64},{96,112},{112,96},{1... | collective-permute-start | bytes 80 | tf_op jit(solution)/shard_map/ppermute | solution.py:8
  267.6 0.8 collective-permute-done.14
  269.2 1.8 collective-permute-done.15
  271.1 1.1 collective-permute-start.16
  272.2 1.3 collective-permute-done.16
  273.5 2.6 collective-permute-start.17
  276.1 1.3 collective-permute-done.17
  283.3 25.1 %all_gather.7 = f32[256,512]{1,0:T(8,128)S(1)} all-gather(f32[16,512]{1,0:T(8,128)S(1)} %multiply_add_fusion.7), channel_id=1, replica_groups=mesh['rep'=16,'fsdp'=16] {'rep'}, dimensions={0}, use_global_device_ids=true | all-gather | bytes 557056 | tf_op jit(solution)/shard_map/all_gather | solution.py:72
  308.4 21.0 %all_gather.6 = f32[128,1792]{1,0:T(8,128)S(1)} all-gather(f32[8,1792]{1,0:T(8,128)S(1)} %multiply_add_fusion.6), channel_id=1, replica_groups=mesh['rep'=16,'fsdp'=16] {'rep'}, dimensions={0}, use_global_device_ids=true | all-gather | bytes 974848 | tf_op jit(solution)/shard_map/all_gather | solution.py:71
  329.5 1.4 multiply_subtract_fusion.1
  331.7 2.0 multiply_subtract_fusion
  333.7 0.9 copy.18
  334.6 0.8 copy.19
  (67 shorter events, 9.6 us)
Async XLA Ops:
  0.6 4.9 %copy-start.1 = (f32[1,256,512]{2,1,0:T(8,128)S(1)}, f32[1,256,512]{2,1,0:T(8,128)}, u32[]{:S(2)}) copy-start(f32[1,256,512]{2,1,0:T(8,128)} %param.9) | copy-start | bytes 1572868
  0.7 20.3 %copy-start = (f32[1,128,1792]{2,1,0:T(8,128)S(1)}, f32[1,128,1792]{2,1,0:T(8,128)}, u32[]{:S(2)}) copy-start(f32[1,128,1792]{2,1,0:T(8,128)} %param.8) | copy-start | bytes 2752516
  1.8 19.2 %collective-permute-start = (f32[64,1792]{1,0:T(8,128)S(1)}, f32[64,1792]{1,0:T(8,128)S(1)}, u32[]{:S(2)}, u32[]{:S(2)}) collective-permute-start(f32[64,1792]{1,0:T(8,128)S(1)} %dynamic-slice_bitcast_fusion), channel_id=1, source_target_pairs={{0,128},{16,144},{32,160},{48,176},{64,192},{80,208},{96,224},{112... | collective-permute-start | bytes 1376264 | tf_op jit(solution)/shard_map/ppermute | solution.py:8
  5.5 14.8 %collective-permute-start.1 = (f32[128,512]{1,0:T(8,128)S(1)}, f32[128,512]{1,0:T(8,128)S(1)}, u32[]{:S(2)}, u32[]{:S(2)}) collective-permute-start(f32[128,512]{1,0:T(8,128)S(1)} %dynamic-slice_bitcast_fusion.1), channel_id=1, source_target_pairs={{0,128},{16,144},{32,160},{48,176},{64,192},{80,208},{96,224},{112... | collective-permute-start | bytes 786440 | tf_op jit(solution)/shard_map/ppermute | solution.py:8
  67.5 4.0 %collective-permute-start.2 = (f32[2,3]{1,0:T(2,128)S(1)}, f32[2,3]{1,0:T(2,128)S(1)}, u32[]{:S(2)}, u32[]{:S(2)}) collective-permute-start(f32[2,3]{1,0:T(2,128)S(1)} %psum.28), channel_id=1, source_target_pairs={{0,128},{16,144},{32,160},{48,176},{64,192},{80,208},{96,224},{112... | collective-permute-start | bytes 80 | tf_op jit(solution)/shard_map/ppermute | solution.py:8
  77.6 3.9 %collective-permute-start.4 = (f32[64,512]{1,0:T(8,128)S(1)}, f32[64,512]{1,0:T(8,128)S(1)}, u32[]{:S(2)}, u32[]{:S(2)}) collective-permute-start(f32[64,512]{1,0:T(8,128)S(1)} %constant_dynamic-slice_fusion.4), channel_id=1, source_target_pairs={{0,64},{16,80},{32,96},{48,112},{64,0},{80,16},{96,32},{112,48},{1... | collective-permute-start | bytes 393224 | tf_op jit(solution)/shard_map/ppermute | solution.py:8
  79.0 5.2 %collective-permute-start.3 = (f32[32,1792]{1,0:T(8,128)S(1)}, f32[32,1792]{1,0:T(8,128)S(1)}, u32[]{:S(2)}, u32[]{:S(2)}) collective-permute-start(f32[32,1792]{1,0:T(8,128)S(1)} %constant_dynamic-slice_fusion.5), channel_id=1, source_target_pairs={{0,64},{16,80},{32,96},{48,112},{64,0},{80,16},{96,32},{112,48},{1... | collective-permute-start | bytes 688136 | tf_op jit(solution)/shard_map/ppermute | solution.py:8
  119.0 2.8 collective-permute-start.5
  121.9 4.2 %collective-permute-start.6 = (f32[2,3]{1,0:T(2,128)S(1)}, f32[2,3]{1,0:T(2,128)S(1)}, u32[]{:S(2)}, u32[]{:S(2)}) collective-permute-start(f32[2,3]{1,0:T(2,128)S(1)} %maximum_add_fusion.1), channel_id=1, source_target_pairs={{0,128},{16,144},{32,160},{48,176},{64,192},{80,208},{96,224},{112... | collective-permute-start | bytes 80 | tf_op jit(solution)/shard_map/ppermute | solution.py:8
  132.1 3.5 %collective-permute-start.8 = (f32[32,512]{1,0:T(8,128)S(1)}, f32[32,512]{1,0:T(8,128)S(1)}, u32[]{:S(2)}, u32[]{:S(2)}) collective-permute-start(f32[32,512]{1,0:T(8,128)S(1)} %constant_dynamic-slice_fusion.2), channel_id=1, source_target_pairs={{0,32},{16,48},{32,0},{48,16},{64,96},{80,112},{96,64},{112,80},{1... | collective-permute-start | bytes 196616 | tf_op jit(solution)/shard_map/ppermute | solution.py:8
  132.9 5.3 %collective-permute-start.7 = (f32[16,1792]{1,0:T(8,128)S(1)}, f32[16,1792]{1,0:T(8,128)S(1)}, u32[]{:S(2)}, u32[]{:S(2)}) collective-permute-start(f32[16,1792]{1,0:T(8,128)S(1)} %constant_dynamic-slice_fusion.3), channel_id=1, source_target_pairs={{0,32},{16,48},{32,0},{48,16},{64,96},{80,112},{96,64},{112,80},{1... | collective-permute-start | bytes 344072 | tf_op jit(solution)/shard_map/ppermute | solution.py:8
  174.8 2.8 collective-permute-start.9
  177.7 2.7 collective-permute-start.10
  180.5 3.9 %collective-permute-start.11 = (f32[2,3]{1,0:T(2,128)S(1)}, f32[2,3]{1,0:T(2,128)S(1)}, u32[]{:S(2)}, u32[]{:S(2)}) collective-permute-start(f32[2,3]{1,0:T(2,128)S(1)} %fusion.19), channel_id=1, source_target_pairs={{0,128},{16,144},{32,160},{48,176},{64,192},{80,208},{96,224},{112... | collective-permute-start | bytes 80 | tf_op jit(solution)/shard_map/ppermute | solution.py:8
  190.3 32.5 %collective-permute-start.13 = (f32[16,512]{1,0:T(8,128)S(1)}, f32[16,512]{1,0:T(8,128)S(1)}, u32[]{:S(2)}, u32[]{:S(2)}) collective-permute-start(f32[16,512]{1,0:T(8,128)S(1)} %constant_dynamic-slice_fusion), channel_id=1, source_target_pairs={{0,16},{16,0},{32,48},{48,32},{64,80},{80,64},{96,112},{112,96},{1... | collective-permute-start | bytes 98312 | tf_op jit(solution)/shard_map/ppermute | solution.py:8
  222.0 3.5 %collective-permute-start.12 = (f32[8,1792]{1,0:T(8,128)S(1)}, f32[8,1792]{1,0:T(8,128)S(1)}, u32[]{:S(2)}, u32[]{:S(2)}) collective-permute-start(f32[8,1792]{1,0:T(8,128)S(1)} %constant_dynamic-slice_fusion.1), channel_id=1, source_target_pairs={{0,16},{16,0},{32,48},{48,32},{64,80},{80,64},{96,112},{112,96},{1... | collective-permute-start | bytes 172040 | tf_op jit(solution)/shard_map/ppermute | solution.py:8
  260.3 8.1 %collective-permute-start.14 = (f32[2,3]{1,0:T(2,128)S(1)}, f32[2,3]{1,0:T(2,128)S(1)}, u32[]{:S(2)}, u32[]{:S(2)}) collective-permute-start(f32[2,3]{1,0:T(2,128)S(1)} %psum.31), channel_id=1, source_target_pairs={{0,16},{16,0},{32,48},{48,32},{64,80},{80,64},{96,112},{112,96},{1... | collective-permute-start | bytes 80 | tf_op jit(solution)/shard_map/ppermute | solution.py:8
  268.5 2.4 collective-permute-start.15
  271.1 2.4 collective-permute-start.16
  273.5 3.9 %collective-permute-start.17 = (f32[2,3]{1,0:T(2,128)S(1)}, f32[2,3]{1,0:T(2,128)S(1)}, u32[]{:S(2)}, u32[]{:S(2)}) collective-permute-start(f32[2,3]{1,0:T(2,128)S(1)} %add.191), channel_id=1, source_target_pairs={{0,128},{16,144},{32,160},{48,176},{64,192},{80,208},{96,224},{112... | collective-permute-start | bytes 80 | tf_op jit(solution)/shard_map/ppermute | solution.py:8
  283.3 46.1 %copy-start.7 = (f32[256,512]{1,0:T(8,128)S(1)}, f32[256,512]{1,0:T(8,128)}, u32[]{:S(2)}) copy-start(f32[256,512]{1,0:T(8,128)} %param.15) | copy-start | bytes 1572868
  308.3 21.1 %copy-start.6 = (f32[256,512]{1,0:T(8,128)S(1)}, f32[256,512]{1,0:T(8,128)}, u32[]{:S(2)}) copy-start(f32[256,512]{1,0:T(8,128)} %param.14) | copy-start | bytes 1572868
  308.4 21.1 %copy-start.5 = (f32[256,512]{1,0:T(8,128)S(1)}, f32[256,512]{1,0:T(8,128)}, u32[]{:S(2)}) copy-start(f32[256,512]{1,0:T(8,128)} %param.13) | copy-start | bytes 1572868
  329.4 1.5 copy-start.2
  329.4 2.0 copy-start.3
  329.5 2.3 copy-start.4
where the time goes:
time: 336 us; the launch traced here: 335 us
  blocking collectives  186 us (55%)
  starting transfers between devices  62.1 us (18%)
  waiting for transfers between devices  33.3 us (10%)
  other arithmetic  25.5 us (8%)
  between operations  21.8 us (6%)
  local copies, waits for them, and re-layouts  6.56 us (2%)
    psum x4, blocking collectives, group_sums(): running = lax.psum(partials, 'fsdp')  140 us
    ppermute x18, starting transfers between devices, swapped(): lax.ppermute(x, axis, [(i, i ^ 1 << bit) for i in range(lax.axis_size(axi...  62.1 us
    ppermute x18, waiting for transfers between devices, swapped(): lax.ppermute(x, axis, [(i, i ^ 1 << bit) for i in range(lax.axis_size(axi...  33.3 us
    all_gather x1, blocking collectives, local(): lax.all_gather(holdings[1], 'rep', axis=0, tiled=True)  25.1 us
    all_gather x1, blocking collectives, local(): lax.all_gather(holdings[0], 'rep', axis=0, tiled=True)  21 us
    another operation x11, other arithmetic, local(): partials = jnp.stack(rows_list)  16.1 us
  transfers between devices with their start and end apart: 18, of which 14 were waited for; matrix products, arithmetic and copies ran while one was open for 3% of the time, Pallas kernels for 0%

commit v1 on v0

v1 whole, which is shorter than its diff:
```python
import functools

import jax
import jax.numpy as jnp
from jax import lax
from jax.experimental import pallas as pl
from jax.experimental.pallas import tpu as pltpu
from jax.sharding import PartitionSpec as P

MESH = pl.DeviceIdType.MESH
LANES = 128
SUBS = 8


def adamw_rows(gradient, weights, moment_one, moment_two):
    new_one = 0.9 * moment_one + 0.1 * gradient
    new_two = 0.95 * moment_two + 0.05 * gradient * gradient
    corrected_one = new_one / (1.0 - 0.9**10)
    corrected_two = new_two / (1.0 - 0.95**10)
    step_size = corrected_one / (jnp.sqrt(corrected_two) + 1e-08) + 0.1 * weights
    return (weights - 0.05 * step_size, new_one, new_two)


def lane_xor(value, mask):
    lane = lax.broadcasted_iota(jnp.int32, value.shape, 1)
    up = pltpu.roll(value, LANES - mask, 1)
    down = pltpu.roll(value, mask, 1)
    return jnp.where((lane // mask) % 2 == 0, up, down)


def partner_table(row, masks):
    sub = lax.broadcasted_iota(jnp.int32, row.shape, 0)
    table = row
    for mask in masks:
        table = jnp.where((sub // mask) % 2 == 1, lane_xor(table, mask), table)
    return table


def coefficients(total):
    shape = (SUBS, LANES)
    low = total
    high = pltpu.roll(total, LANES - 32, 1)
    result = None
    for mask in (8, 4, 2, 1):
        own = jnp.broadcast_to(low[0:1, :], shape)
        cross = jnp.broadcast_to(high[0:1, :], shape)
        coef = 1.0 - cross / (2.0 * own)
        result = coef if result is None else result * coef
        if mask == 1:
            break
        other = lane_xor(coef, mask)
        table = partner_table(coef, [bit for bit in (1, 2, 4) if bit < mask])
        table_other = lane_xor(table, mask)
        low = (
            coef * (table * low + table_other * high)
            + other * (table * lane_xor(high, mask) + table_other * lane_xor(low, mask))
        )
        high = pltpu.roll(low, SUBS - mask // 2, 0)
    return result


def pair_sums(ref, number, sums):
    rows, cols = ref.shape[1], ref.shape[2]
    for first in range(4):
        for second in range(first, 4):

            def body(tile, acc, first=first, second=second):
                at = pl.ds(pl.multiple_of(tile * LANES, LANES), LANES)
                for half in range(rows // SUBS):
                    band = slice(half * SUBS, half * SUBS + SUBS)
                    left = ref[4 * first : 4 * first + 4, band, at]
                    right = ref[4 * second : 4 * second + 4, band, at]
                    acc = acc + left[:, None] * right[None, :]
                return acc

            acc = lax.fori_loop(0, cols // LANES, body, jnp.zeros((4, 4, SUBS, LANES), jnp.float32))
            for u in range(4):
                for w in range(4):
                    i, j = 4 * first + u, 4 * second + w
                    k = i ^ j
                    sums[number, i, k // 8, 8 * (k % 8) : 8 * (k % 8) + 8, :] = acc[u, w]
                    if first != second:
                        sums[number, j, k // 8, 8 * (k % 8) : 8 * (k % 8) + 8, :] = acc[u, w]


def packed_sums(number, sums):
    ones = jnp.ones((LANES, LANES), jnp.float32)
    shape = (16, SUBS, LANES)
    lane = lax.broadcasted_iota(jnp.int32, shape, 2)
    place = lax.broadcasted_iota(jnp.int32, shape, 0)
    packed = None
    for half in range(2):
        rows = None
        for sub in range(SUBS):
            part = sums[number, :, half, pl.ds(sub, SUBS, stride=SUBS), :]
            rows = part if rows is None else rows + part
        full = jnp.dot(
            rows.reshape(16 * SUBS, LANES),
            ones,
            precision=lax.Precision.HIGHEST,
            preferred_element_type=jnp.float32,
        ).reshape(shape)
        spread = jnp.sum(jnp.where(lane == place + (half * 32 + number * 16), full, 0.0), axis=0)
        packed = spread if packed is None else packed + spread
    return packed


def kernel(
    grad_g, grad_d, full_g, full_d,
    recv_g, recv_d, sums, part, slots_a, part_b, slots_b,
    own_sem, send_x, recv_x, send_a, recv_a, send_b, recv_b, send_w, recv_w, send_f,
):
    rep, fs = lax.axis_index("rep"), lax.axis_index("fsdp")
    x, zc = rep // 4, rep % 4
    zl, core = zc // 2, zc % 2
    y, zh = fs // 4, fs % 4

    def rep_id(x_, zc_):
        return (x_ % 4) * 4 + zc_ % 4

    rep_steps = [(dx, dz) for dx in (2, 1, 3, 0) for dz in (2, 3, 1, 0) if (dx, dz) != (0, 0)]
    pair_steps = [(a, b) for a in range(4) for b in range(4) if (a, b) != (0, 0)]

    def plane_id(dx, dy):
        return (rep_id(x + dx, zc), ((y + dy) % 4) * 4 + zh)

    def column_id(dh, dz):
        return (rep_id(x, zc + dz), y * 4 + (zh + dh) % 4)

    barrier = pltpu.get_barrier_semaphore()
    partners = [(rep_id(x + dx, zc + dz), fs) for dx, dz in rep_steps]
    partners += [plane_id(dx, dy) for dx, dy in pair_steps if dy]
    partners += [column_id(dh, dz) for dh, dz in pair_steps if dh]
    for who in partners:
        pl.semaphore_signal(barrier, inc=1, device_id=who, device_id_type=MESH)
    tensors = ((grad_g, recv_g, full_g, 8), (grad_d, recv_d, full_d, 16))
    for number, (grad, recv, _, rows) in enumerate(tensors):
        pltpu.make_async_copy(
            grad.at[pl.ds(rep * rows, rows), :], recv.at[rep], own_sem.at[number]
        ).start()
    pl.semaphore_wait(barrier, len(partners))

    def row_copy(number, dx, dz, outgoing):
        grad, recv, _, rows = tensors[number]
        there = rep_id(x + dx, zc + dz)
        source = rep if outgoing else rep_id(x - dx + 4, zc - dz + 4)
        return pltpu.make_async_remote_copy(
            src_ref=grad.at[pl.ds(there * rows, rows), :],
            dst_ref=recv.at[source],
            send_sem=send_x.at[number, 4 * dx + dz],
            recv_sem=recv_x.at[number, 4 * dx + dz],
            device_id=(there, fs),
            device_id_type=MESH,
        )

    for number in range(2):
        for dx, dz in rep_steps:
            row_copy(number, dx, dz, True).start()

    total = None
    for number, (grad, recv, _, rows) in enumerate(tensors):
        pltpu.make_async_copy(
            grad.at[pl.ds(rep * rows, rows), :], recv.at[rep], own_sem.at[number]
        ).wait()
        for dx, dz in rep_steps:
            row_copy(number, dx, dz, False).wait_recv()
        pair_sums(recv, number, sums)
        packed = packed_sums(number, sums)
        total = packed if total is None else total + packed

    def exchange(value, mine, slots, send, recv, here, reach):
        mine[...] = value
        copies = []
        for a, b in pair_steps:
            copies.append(
                pltpu.make_async_remote_copy(
                    src_ref=mine,
                    dst_ref=slots.at[here],
                    send_sem=send.at[4 * a + b],
                    recv_sem=recv.at[4 * a + b],
                    device_id=reach(a, b),
                    device_id_type=MESH,
                )
            )
        for copy in copies:
            copy.start()
        slots[here] = value
        for copy in copies:
            copy.wait_recv()
        return jnp.sum(slots[...], axis=0), copies

    total, copies_a = exchange(total, part, slots_a, send_a, recv_a, x * 4 + y, plane_id)
    total, copies_b = exchange(total, part_b, slots_b, send_b, recv_b, zh * 4 + zc, column_id)

    coef = coefficients(total)
    for number, (_, recv, full, rows) in enumerate(tensors):
        scale = [coef[0:1, number * 16 + i : number * 16 + i + 1] for i in range(16)]
        cols = recv.shape[2]
        value = None
        for i in range(16):
            term = jnp.broadcast_to(scale[i], (rows, cols)) * recv[i]
            value = term if value is None else value + term
        full[pl.ds(pl.multiple_of(rep * rows, rows), rows), :] = value

    def give(number, source, there, send, recv):
        _, _, full, rows = tensors[number]
        at = full.at[pl.ds(source * rows, rows), :]
        return pltpu.make_async_remote_copy(
            src_ref=at, dst_ref=at, send_sem=send, recv_sem=recv,
            device_id=(there, fs), device_id_type=MESH,
        )

    def chip(dx, dl, c):
        return ((x + dx) % 4) * 4 + ((zl + dl) % 2) * 2 + c

    chips = [(dx, dl) for dx in (2, 1, 3, 0) for dl in (1, 0) if (dx, dl) != (0, 0)]
    arrivals = [(0, 1), (1, 0), (3, 0), (1, 1), (3, 1), (2, 0), (2, 1)]
    sibling = zl * 2 + 1 - core + x * 4
    sends = []
    for number in range(2):
        for dx, dl in chips:
            slot = 2 * dx + dl
            sends.append(give(number, rep, chip(dx, dl, core), send_w.at[number, slot], recv_w.at[number, slot]))
        sends.append(give(number, rep, sibling, send_w.at[number, 0], recv_w.at[number, 8]))
    for copy in sends:
        copy.start()
    for number in range(2):
        for dx, dl in arrivals:
            slot = 2 * dx + dl
            source = chip(4 - dx, 2 - dl, core)
            give(number, source, sibling, send_w.at[number, slot], recv_w.at[number, slot]).wait_recv()
            copy = give(number, source, sibling, send_f.at[number, slot], recv_w.at[number, 8 + slot])
            copy.start()
            sends.append(copy)
    for number in range(2):
        for dx, dl in [(0, 0)] + arrivals:
            slot = 2 * dx + dl
            source = chip(4 - dx, 2 - dl, 1 - core)
            give(number, source, sibling, send_f.at[number, slot], recv_w.at[number, 8 + slot]).wait_recv()
    for number in range(2):
        for dx, dz in rep_steps:
            row_copy(number, dx, dz, True).wait_send()
    for copy in copies_a + copies_b + sends:
        copy.wait_send()


def combined(grad_g, grad_d):
    f32 = jnp.float32
    rows_g, cols_g = grad_g.shape
    rows_d, cols_d = grad_d.shape
    dma = pltpu.SemaphoreType.DMA
    return pl.pallas_call(
        kernel,
        out_shape=(
            jax.ShapeDtypeStruct(grad_g.shape, f32),
            jax.ShapeDtypeStruct(grad_d.shape, f32),
        ),
        in_specs=[pl.BlockSpec(memory_space=pl.ANY)] * 2,
        out_specs=[pl.BlockSpec(memory_space=pltpu.VMEM)] * 2,
        scratch_shapes=[
            pltpu.VMEM((16, rows_g // 16, cols_g), f32),
            pltpu.VMEM((16, rows_d // 16, cols_d), f32),
            pltpu.VMEM((2, 16, 2, 64, LANES), f32),
            pltpu.VMEM((SUBS, LANES), f32),
            pltpu.VMEM((16, SUBS, LANES), f32),
            pltpu.VMEM((SUBS, LANES), f32),
            pltpu.VMEM((16, SUBS, LANES), f32),
            dma((2,)),
            dma((2, 16)),
            dma((2, 16)),
            dma((16,)),
            dma((16,)),
            dma((16,)),
            dma((16,)),
            dma((2, 8)),
            dma((2, 16)),
            dma((2, 8)),
        ],
        compiler_params=pltpu.CompilerParams(
            collective_id=0, has_side_effects=True, vmem_limit_bytes=20 << 20
        ),
        name="adasum",
    )(grad_g, grad_d)


def local(grad_gate, grad_down, param_gate, mom1_gate, mom2_gate, param_down, mom1_down, mom2_down):
    full_gate, full_down = combined(grad_gate[0], grad_down[0])
    gate_param, gate_one, gate_two = adamw_rows(full_gate, param_gate, mom1_gate, mom2_gate)
    down_param, down_one, down_two = adamw_rows(full_down, param_down, mom1_down, mom2_down)
    return (full_gate, gate_param, gate_one, gate_two, full_down, down_param, down_one, down_two)


def solution(mesh):
    whole, part = P("rep", None, "fsdp"), P(None, "fsdp")
    return jax.shard_map(
        local, mesh=mesh, in_specs=(whole, whole) + (part,) * 6, out_specs=(part,) * 8, check_vma=False
    )
```

time: 336 us -> 62.9 us (0.19)
  blocking collectives: 186 us -> 0 us
  starting transfers between devices: 62.1 us -> 0 us
  Pallas kernels: 0 us -> 53.2 us
  waiting for transfers between devices: 33.3 us -> 0 us
  between operations: 21.8 us -> 0.69 us
  other arithmetic: 25.5 us -> 4.94 us
    psum x4 -> x0, blocking collectives: 140 us -> none  [group_sums(): running = lax.psum(partials, 'fsdp')]
    ppermute x18 -> x0, starting transfers between devices: 62.1 us -> none  [swapped(): lax.ppermute(x, axis, [(i, i ^ 1 << bit) for i in range(lax.axis_size(axi...]
    pallas_call x0 -> x1, Pallas kernels: none -> 53.2 us  [combined(): pl.pallas_call(kernel, out_shape=(jax.ShapeDtypeStruct(grad_g.shape, f32)...]
    all_gather x2 -> x0, blocking collectives: 46.1 us -> none  [the longest x1 25.1 us: local(): lax.all_gather(holdings[1], 'rep', axis=0, tiled=True)]
    ppermute x18 -> x0, waiting for transfers between devices: 33.3 us -> none  [swapped(): lax.ppermute(x, axis, [(i, i ^ 1 << bit) for i in range(lax.axis_size(axi...]
    another operation x11 -> x0, other arithmetic: 16.1 us -> none  [local(): partials = jnp.stack(rows_list)]
    reduce_sum x8 -> x0, other arithmetic: 5.28 us -> none  [local(): jnp.sum(mine_part * their_part)]
  transfers between devices with their start and end apart: 18 -> 0, of which waited for: 14 -> 0; matrix products, arithmetic and copies ran while one was open for 3% -> 0% of each run, Pallas kernels for 0% -> 0%
where the time goes in v1:
time: 62.9 us; the launch traced here: 62.7 us
  Pallas kernels  53.2 us (85%)
  other arithmetic  4.94 us (8%)
  local copies, waits for them, and re-layouts  3.95 us (6%)
  between operations  0.69 us (1%)
    pallas_call x1, Pallas kernels, combined(): pl.pallas_call(kernel, out_shape=(jax.ShapeDtypeStruct(grad_g.shape, f32)...  53.2 us
    sub x2, other arithmetic, adamw_rows(): return (weights - 0.05 * step_size, new_one, new_two)  4.94 us
    unnamed x14, local copies, waits for them, and re-layouts  3.95 us

profile of v1, /device:TPU:1, one launch (start us, length us, event | category | flops | bytes accessed | tf_op | source)
XLA Modules:
  0.0 62.7 jit_solution(5344509933351158379)
XLA Ops:
  0.6 0.0 copy-start
  0.6 1.2 %copy-done = f32[1,128,1792]{2,1,0:T(8,128)S(1)} copy-done((f32[1,128,1792]{2,1,0:T(8,128)S(1)}, f32[1,128,1792]{2,1,0:T(8,128)}, u32[]{:S(2)}) %copy-start) | copy-done | bytes 917528
  1.8 0.0 copy-start.1
  1.8 1.0 %copy-done.1 = f32[1,256,512]{2,1,0:T(8,128)S(1)} copy-done((f32[1,256,512]{2,1,0:T(8,128)S(1)}, f32[1,256,512]{2,1,0:T(8,128)}, u32[]{:S(2)}) %copy-start.1) | copy-done | bytes 524312
  2.9 0.0 copy-start.2
  2.9 53.2 %adasum.1 = (f32[128,1792]{1,0:T(8,128)S(1)}, f32[256,512]{1,0:T(8,128)S(1)}) custom-call(f32[128,1792]{1,0:T(8,128)S(1)} %bitcast.2, f32[256,512]{1,0:T(8,128)S(1)} %bitcast.3), custom_call_target="tpu_custom_call" | custom-call | tf_op jit(solution)/shard_map/adasum/pallas_call | solution.py:252
  56.0 0.0 copy-done.2
  56.0 0.0 copy-start.3
  56.0 0.0 copy-start.4
  56.1 0.0 copy-start.5
  56.1 3.5 %multiply_subtract_fusion = (f32[128,1792]{1,0:T(8,128)}, f32[128,1792]{1,0:T(8,128)}, f32[128,1792]{1,0:T(8,128)}) fusion(f32[128,1792]{1,0:T(8,128)S(1)} %copy-done.2, f32[128,1792]{1,0:T(8,128)S(1)} %get-tuple-element.26, f32[128,1792]{1,0:T(8,128)} %param.11, f32[128,1792]{1,0:T(8,128)} %param.12), kind=kLoop, calls=%fused_computation.2 | loop fusion | flops 3440640 | bytes 6422528 | tf_op jit(solution)/shard_map/sub | solution.py:21
  59.6 0.0 copy-done.3
  59.6 0.0 copy-done.4
  59.6 0.0 copy-done.5
  59.6 1.4 %multiply_subtract_fusion.1 = (f32[256,512]{1,0:T(8,128)}, f32[256,512]{1,0:T(8,128)}, f32[256,512]{1,0:T(8,128)}) fusion(f32[256,512]{1,0:T(8,128)S(1)} %copy-done.3, f32[256,512]{1,0:T(8,128)S(1)} %get-tuple-element.30, f32[256,512]{1,0:T(8,128)S(1)} %copy-done.4, f32[256,512]{1,0:T(8,128)S(1)} %copy-done.5), kind=kLoop, calls=%fused_computation.6 | loop fusion | flops 1966080 | bytes 3670016 | tf_op jit(solution)/shard_map/sub | solution.py:21
  61.0 0.9 %copy.18 = f32[128,1792]{1,0:T(8,128)} copy(f32[128,1792]{1,0:T(8,128)S(1)} %get-tuple-element.26) | data formatting | bytes 1835008
  61.9 0.8 %copy.19 = f32[256,512]{1,0:T(8,128)} copy(f32[256,512]{1,0:T(8,128)S(1)} %get-tuple-element.30) | data formatting | bytes 1048576
Async XLA Ops:
  0.6 1.2 %copy-start = (f32[1,128,1792]{2,1,0:T(8,128)S(1)}, f32[1,128,1792]{2,1,0:T(8,128)}, u32[]{:S(2)}) copy-start(f32[1,128,1792]{2,1,0:T(8,128)} %param.8) | copy-start | bytes 2752516
  1.8 1.0 %copy-start.1 = (f32[1,256,512]{2,1,0:T(8,128)S(1)}, f32[1,256,512]{2,1,0:T(8,128)}, u32[]{:S(2)}) copy-start(f32[1,256,512]{2,1,0:T(8,128)} %param.9) | copy-start | bytes 1572868
  2.9 53.2 %copy-start.2 = (f32[128,1792]{1,0:T(8,128)S(1)}, f32[128,1792]{1,0:T(8,128)}, u32[]{:S(2)}) copy-start(f32[128,1792]{1,0:T(8,128)} %param.10) | copy-start | bytes 2752516
  56.0 3.6 %copy-start.3 = (f32[256,512]{1,0:T(8,128)S(1)}, f32[256,512]{1,0:T(8,128)}, u32[]{:S(2)}) copy-start(f32[256,512]{1,0:T(8,128)} %param.13) | copy-start | bytes 1572868
  56.0 3.6 %copy-start.4 = (f32[256,512]{1,0:T(8,128)S(1)}, f32[256,512]{1,0:T(8,128)}, u32[]{:S(2)}) copy-start(f32[256,512]{1,0:T(8,128)} %param.14) | copy-start | bytes 1572868
  56.1 3.5 %copy-start.5 = (f32[256,512]{1,0:T(8,128)S(1)}, f32[256,512]{1,0:T(8,128)}, u32[]{:S(2)}) copy-start(f32[256,512]{1,0:T(8,128)} %param.15) | copy-start | bytes 1572868

commit v2 on v1

--- a/solution.py
+++ b/solution.py
@@ -1,5 +1,3 @@
-import functools
-
 import jax
 import jax.numpy as jnp
 from jax import lax
@@ -157,48 +155,56 @@
         for dx, dz in rep_steps:
             row_copy(number, dx, dz, True).start()
 
-    total = None
-    for number, (grad, recv, _, rows) in enumerate(tensors):
+    def inner(number):
+        grad, recv, _, rows = tensors[number]
         pltpu.make_async_copy(
             grad.at[pl.ds(rep * rows, rows), :], recv.at[rep], own_sem.at[number]
         ).wait()
         for dx, dz in rep_steps:
             row_copy(number, dx, dz, False).wait_recv()
         pair_sums(recv, number, sums)
-        packed = packed_sums(number, sums)
-        total = packed if total is None else total + packed
-
-    def exchange(value, mine, slots, send, recv, here, reach):
-        mine[...] = value
-        copies = []
-        for a, b in pair_steps:
-            copies.append(
-                pltpu.make_async_remote_copy(
-                    src_ref=mine,
-                    dst_ref=slots.at[here],
-                    send_sem=send.at[4 * a + b],
-                    recv_sem=recv.at[4 * a + b],
-                    device_id=reach(a, b),
-                    device_id_type=MESH,
-                )
+        return packed_sums(number, sums)
+
+    stages = (
+        (part, slots_a, send_a, recv_a, x * 4 + y, plane_id),
+        (part_b, slots_b, send_b, recv_b, zh * 4 + zc, column_id),
+    )
+    sends = []
+
+    def spread(number, stage, value):
+        mine, slots, send, recv, here, reach = stages[stage]
+        mine[number] = value
+        copies = [
+            pltpu.make_async_remote_copy(
+                src_ref=mine.at[number],
+                dst_ref=slots.at[number, here],
+                send_sem=send.at[number, 4 * a + b],
+                recv_sem=recv.at[number, 4 * a + b],
+                device_id=reach(a, b),
+                device_id_type=MESH,
             )
+            for a, b in pair_steps
+        ]
         for copy in copies:
             copy.start()
-        slots[here] = value
-        for copy in copies:
-            copy.wait_recv()
-        return jnp.sum(slots[...], axis=0), copies
-
-    total, copies_a = exchange(total, part, slots_a, send_a, recv_a, x * 4 + y, plane_id)
-    total, copies_b = exchange(total, part_b, slots_b, send_b, recv_b, zh * 4 + zc, column_id)
-
-    coef = coefficients(total)
-    for number, (_, recv, full, rows) in enumerate(tensors):
-        scale = [coef[0:1, number * 16 + i : number * 16 + i + 1] for i in range(16)]
+        slots[number, here] = value
+        sends.extend(copies)
+
+        def collect():
+            for copy in copies:
+                copy.wait_recv()
+            return jnp.sum(slots[number], axis=0)
+
+        return collect
+
+    def combine(number, total):
+        _, recv, full, rows = tensors[number]
+        coef = coefficients(total)
         cols = recv.shape[2]
         value = None
         for i in range(16):
-            term = jnp.broadcast_to(scale[i], (rows, cols)) * recv[i]
+            at = number * 16 + i
+            term = jnp.broadcast_to(coef[0:1, at : at + 1], (rows, cols)) * recv[i]
             value = term if value is None else value + term
         full[pl.ds(pl.multiple_of(rep * rows, rows), rows), :] = value
 
@@ -216,14 +222,25 @@
     chips = [(dx, dl) for dx in (2, 1, 3, 0) for dl in (1, 0) if (dx, dl) != (0, 0)]
     arrivals = [(0, 1), (1, 0), (3, 0), (1, 1), (3, 1), (2, 0), (2, 1)]
     sibling = zl * 2 + 1 - core + x * 4
-    sends = []
-    for number in range(2):
+
+    def give_own(number):
+        copies = []
         for dx, dl in chips:
             slot = 2 * dx + dl
-            sends.append(give(number, rep, chip(dx, dl, core), send_w.at[number, slot], recv_w.at[number, slot]))
-        sends.append(give(number, rep, sibling, send_w.at[number, 0], recv_w.at[number, 8]))
-    for copy in sends:
-        copy.start()
+            copies.append(give(number, rep, chip(dx, dl, core), send_w.at[number, slot], recv_w.at[number, slot]))
+        copies.append(give(number, rep, sibling, send_w.at[number, 0], recv_w.at[number, 8]))
+        for copy in copies:
+            copy.start()
+        sends.extend(copies)
+
+    gate = spread(0, 0, inner(0))
+    gate = spread(0, 1, gate())
+    down = spread(1, 0, inner(1))
+    combine(0, gate())
+    give_own(0)
+    down = spread(1, 1, down())
+    combine(1, down())
+    give_own(1)
     for number in range(2):
         for dx, dl in arrivals:
             slot = 2 * dx + dl
@@ -240,7 +257,7 @@
     for number in range(2):
         for dx, dz in rep_steps:
             row_copy(number, dx, dz, True).wait_send()
-    for copy in copies_a + copies_b + sends:
+    for copy in sends:
         copy.wait_send()
 
 
@@ -261,17 +278,17 @@
             pltpu.VMEM((16, rows_g // 16, cols_g), f32),
             pltpu.VMEM((16, rows_d // 16, cols_d), f32),
             pltpu.VMEM((2, 16, 2, 64, LANES), f32),
-            pltpu.VMEM((SUBS, LANES), f32),
-            pltpu.VMEM((16, SUBS, LANES), f32),
-            pltpu.VMEM((SUBS, LANES), f32),
-            pltpu.VMEM((16, SUBS, LANES), f32),
+            pltpu.VMEM((2, SUBS, LANES), f32),
+            pltpu.VMEM((2, 16, SUBS, LANES), f32),
+            pltpu.VMEM((2, SUBS, LANES), f32),
+            pltpu.VMEM((2, 16, SUBS, LANES), f32),
             dma((2,)),
             dma((2, 16)),
             dma((2, 16)),
-            dma((16,)),
-            dma((16,)),
-            dma((16,)),
-            dma((16,)),
+            dma((2, 16)),
+            dma((2, 16)),
+            dma((2, 16)),
+            dma((2, 16)),
             dma((2, 8)),
             dma((2, 16)),
             dma((2, 8)),

time: 62.9 us -> 67.3 us (1.070)
  Pallas kernels: 53.2 us -> 57.5 us
    pallas_call x1, Pallas kernels: 53.2 us -> 57.5 us  [combined(): pl.pallas_call(kernel, out_shape=(jax.ShapeDtypeStruct(grad_g.shape, f32)...]
where the time goes in v2:
time: 67.3 us; the launch traced here: 67.1 us
  Pallas kernels  57.5 us (85%)
  other arithmetic  4.94 us (7%)
  local copies, waits for them, and re-layouts  3.95 us (6%)
  between operations  0.69 us (1%)
    pallas_call x1, Pallas kernels, combined(): pl.pallas_call(kernel, out_shape=(jax.ShapeDtypeStruct(grad_g.shape, f32)...  57.5 us
    sub x2, other arithmetic, adamw_rows(): return (weights - 0.05 * step_size, new_one, new_two)  4.94 us
    unnamed x14, local copies, waits for them, and re-layouts  3.95 us

profile of v2, /device:TPU:1, one launch (start us, length us, event | category | flops | bytes accessed | tf_op | source)
XLA Modules:
  0.0 67.1 jit_solution(1369181295174504454)
XLA Ops:
  0.6 0.0 copy-start
  0.6 1.2 %copy-done = f32[1,128,1792]{2,1,0:T(8,128)S(1)} copy-done((f32[1,128,1792]{2,1,0:T(8,128)S(1)}, f32[1,128,1792]{2,1,0:T(8,128)}, u32[]{:S(2)}) %copy-start) | copy-done | bytes 917528
  1.8 0.0 copy-start.1
  1.8 1.0 %copy-done.1 = f32[1,256,512]{2,1,0:T(8,128)S(1)} copy-done((f32[1,256,512]{2,1,0:T(8,128)S(1)}, f32[1,256,512]{2,1,0:T(8,128)}, u32[]{:S(2)}) %copy-start.1) | copy-done | bytes 524312
  2.9 0.0 copy-start.2
  2.9 57.5 %adasum.1 = (f32[128,1792]{1,0:T(8,128)S(1)}, f32[256,512]{1,0:T(8,128)S(1)}) custom-call(f32[128,1792]{1,0:T(8,128)S(1)} %bitcast.2, f32[256,512]{1,0:T(8,128)S(1)} %bitcast.3), custom_call_target="tpu_custom_call" | custom-call | tf_op jit(solution)/shard_map/adasum/pallas_call | solution.py:269
  60.4 0.0 copy-done.2
  60.4 0.0 copy-start.3
  60.4 0.0 copy-start.4
  60.4 0.0 copy-start.5
  60.5 3.5 %multiply_subtract_fusion = (f32[128,1792]{1,0:T(8,128)}, f32[128,1792]{1,0:T(8,128)}, f32[128,1792]{1,0:T(8,128)}) fusion(f32[128,1792]{1,0:T(8,128)S(1)} %copy-done.2, f32[128,1792]{1,0:T(8,128)S(1)} %get-tuple-element.26, f32[128,1792]{1,0:T(8,128)} %param.11, f32[128,1792]{1,0:T(8,128)} %param.12), kind=kLoop, calls=%fused_computation.2 | loop fusion | flops 3440640 | bytes 6422528 | tf_op jit(solution)/shard_map/sub | solution.py:19
  64.0 0.0 copy-done.3
  64.0 0.0 copy-done.4
  64.0 0.0 copy-done.5
  64.0 1.4 %multiply_subtract_fusion.1 = (f32[256,512]{1,0:T(8,128)}, f32[256,512]{1,0:T(8,128)}, f32[256,512]{1,0:T(8,128)}) fusion(f32[256,512]{1,0:T(8,128)S(1)} %copy-done.3, f32[256,512]{1,0:T(8,128)S(1)} %get-tuple-element.30, f32[256,512]{1,0:T(8,128)S(1)} %copy-done.4, f32[256,512]{1,0:T(8,128)S(1)} %copy-done.5), kind=kLoop, calls=%fused_computation.6 | loop fusion | flops 1966080 | bytes 3670016 | tf_op jit(solution)/shard_map/sub | solution.py:19
  65.4 0.9 %copy.18 = f32[128,1792]{1,0:T(8,128)} copy(f32[128,1792]{1,0:T(8,128)S(1)} %get-tuple-element.26) | data formatting | bytes 1835008
  66.3 0.8 %copy.19 = f32[256,512]{1,0:T(8,128)} copy(f32[256,512]{1,0:T(8,128)S(1)} %get-tuple-element.30) | data formatting | bytes 1048576
Async XLA Ops:
  0.6 1.2 %copy-start = (f32[1,128,1792]{2,1,0:T(8,128)S(1)}, f32[1,128,1792]{2,1,0:T(8,128)}, u32[]{:S(2)}) copy-start(f32[1,128,1792]{2,1,0:T(8,128)} %param.8) | copy-start | bytes 2752516
  1.8 1.0 %copy-start.1 = (f32[1,256,512]{2,1,0:T(8,128)S(1)}, f32[1,256,512]{2,1,0:T(8,128)}, u32[]{:S(2)}) copy-start(f32[1,256,512]{2,1,0:T(8,128)} %param.9) | copy-start | bytes 1572868
  2.9 57.6 %copy-start.2 = (f32[128,1792]{1,0:T(8,128)S(1)}, f32[128,1792]{1,0:T(8,128)}, u32[]{:S(2)}) copy-start(f32[128,1792]{1,0:T(8,128)} %param.10) | copy-start | bytes 2752516
  60.4 3.6 %copy-start.3 = (f32[256,512]{1,0:T(8,128)S(1)}, f32[256,512]{1,0:T(8,128)}, u32[]{:S(2)}) copy-start(f32[256,512]{1,0:T(8,128)} %param.13) | copy-start | bytes 1572868
  60.4 3.6 %copy-start.4 = (f32[256,512]{1,0:T(8,128)S(1)}, f32[256,512]{1,0:T(8,128)}, u32[]{:S(2)}) copy-start(f32[256,512]{1,0:T(8,128)} %param.14) | copy-start | bytes 1572868
  60.4 3.5 %copy-start.5 = (f32[256,512]{1,0:T(8,128)S(1)}, f32[256,512]{1,0:T(8,128)}, u32[]{:S(2)}) copy-start(f32[256,512]{1,0:T(8,128)} %param.15) | copy-start | bytes 1572868

commit v3 on v1

--- a/solution.py
+++ b/solution.py
@@ -1,5 +1,3 @@
-import functools
-
 import jax
 import jax.numpy as jnp
 from jax import lax
@@ -277,17 +275,44 @@
             dma((2, 8)),
         ],
         compiler_params=pltpu.CompilerParams(
-            collective_id=0, has_side_effects=True, vmem_limit_bytes=20 << 20
+            collective_id=0, has_side_effects=True, vmem_limit_bytes=59 << 20
         ),
         name="adasum",
     )(grad_g, grad_d)
 
 
-def local(grad_gate, grad_down, param_gate, mom1_gate, mom2_gate, param_down, mom1_down, mom2_down):
-    full_gate, full_down = combined(grad_gate[0], grad_down[0])
-    gate_param, gate_one, gate_two = adamw_rows(full_gate, param_gate, mom1_gate, mom2_gate)
-    down_param, down_one, down_two = adamw_rows(full_down, param_down, mom1_down, mom2_down)
-    return (full_gate, gate_param, gate_one, gate_two, full_down, down_param, down_one, down_two)
+STEPS = 4
+
+
+def update_kernel(full_g, full_d, *refs):
+    states, outs = refs[:6], refs[6:]
+    for number, full in enumerate((full_g, full_d)):
+        rows = full.shape[0] // STEPS
+        gradient = full[...]
+        weights, one, two = (ref[...] for ref in states[3 * number : 3 * number + 3])
+        values = (gradient, *adamw_rows(gradient, weights, one, two))
+        for out, value in zip(outs[4 * number : 4 * number + 4], values):
+            out[...] = value
+
+
+def update(full_g, full_d, *states):
+    def blocks(shapes):
+        return [pl.BlockSpec((rows // STEPS, cols), lambda i: (i, 0)) for rows, cols in shapes]
+
+    shapes = [full_g.shape] * 4 + [full_d.shape] * 4
+    return pl.pallas_call(
+        update_kernel,
+        grid=(STEPS,),
+        out_shape=[jax.ShapeDtypeStruct(shape, jnp.float32) for shape in shapes],
+        in_specs=blocks([a.shape for a in (full_g, full_d, *states)]),
+        out_specs=blocks(shapes),
+        compiler_params=pltpu.CompilerParams(vmem_limit_bytes=59 << 20),
+        name="adamw",
+    )(full_g, full_d, *states)
+
+
+def local(grad_gate, grad_down, *states):
+    return tuple(update(*combined(grad_gate[0], grad_down[0]), *states))
 
 
 def solution(mesh):

time: 62.9 us -> 61.6 us (0.979)
  Pallas kernels: 53.2 us -> 60.8 us
  other arithmetic: 4.94 us -> 0 us
  local copies, waits for them, and re-layouts: 3.95 us -> 0 us
    pallas_call x0 -> x1, Pallas kernels: none -> 6.07 us  [update(): pl.pallas_call(update_kernel, grid=(STEPS,), out_shape=[jax.ShapeDtypeStr...]
    sub x2 -> x0, other arithmetic: 4.94 us -> none  [adamw_rows(): return (weights - 0.05 * step_size, new_one, new_two)]
    unnamed x14 -> x0, local copies, waits for them, and re-layouts: 3.95 us -> none
    pallas_call x1, Pallas kernels: 53.2 us -> 54.7 us  [combined(): pl.pallas_call(kernel, out_shape=(jax.ShapeDtypeStruct(grad_g.shape, f32)...]
where the time goes in v3:
time: 61.6 us; the launch traced here: 61.4 us
  Pallas kernels  60.8 us (99%)
  between operations  0.64 us (1%)
    pallas_call x1, Pallas kernels, combined(): pl.pallas_call(kernel, out_shape=(jax.ShapeDtypeStruct(grad_g.shape, f32)...  54.7 us
    pallas_call x1, Pallas kernels, update(): pl.pallas_call(update_kernel, grid=(STEPS,), out_shape=[jax.ShapeDtypeStr...  6.07 us

profile of v3, /device:TPU:1, one launch (start us, length us, event | category | flops | bytes accessed | tf_op | source)
XLA Modules:
  0.0 61.4 jit_solution(1148346680639996794)
XLA Ops:
  0.6 54.7 %adasum.1 = (f32[128,1792]{1,0:T(8,128)}, f32[256,512]{1,0:T(8,128)}) custom-call(f32[128,1792]{1,0:T(8,128)} %bitcast.2, f32[256,512]{1,0:T(8,128)} %bitcast.3), custom_call_target="tpu_custom_call" | custom-call | tf_op jit(solution)/shard_map/adasum/pallas_call | solution.py:250
  55.3 6.1 %adamw.1 = (f32[128,1792]{1,0:T(8,128)}, f32[128,1792]{1,0:T(8,128)}, f32[128,1792]{1,0:T(8,128)}, f32[128,1792]{1,0:T(8,128)}, f32[256,512]{1,0:T(8,128)}, /*in...) custom-call(f32[128,1792]{1,0:T(8,128)} %get-tuple-element.10.full_g, ...), custom_call_target="tpu_custom_call" | custom-call | tf_op jit(solution)/shard_map/adamw/pallas_call | solution.py:303

commit v4 on v3

--- a/solution.py
+++ b/solution.py
@@ -211,7 +211,7 @@
     def chip(dx, dl, c):
         return ((x + dx) % 4) * 4 + ((zl + dl) % 2) * 2 + c
 
-    chips = [(dx, dl) for dx in (2, 1, 3, 0) for dl in (1, 0) if (dx, dl) != (0, 0)]
+    chips = [(0, 1), (2, 0), (1, 0), (3, 0)]
     arrivals = [(0, 1), (1, 0), (3, 0), (1, 1), (3, 1), (2, 0), (2, 1)]
     sibling = zl * 2 + 1 - core + x * 4
     sends = []
@@ -222,14 +222,26 @@
         sends.append(give(number, rep, sibling, send_w.at[number, 0], recv_w.at[number, 8]))
     for copy in sends:
         copy.start()
-    for number in range(2):
-        for dx, dl in arrivals:
-            slot = 2 * dx + dl
-            source = chip(4 - dx, 2 - dl, core)
-            give(number, source, sibling, send_w.at[number, slot], recv_w.at[number, slot]).wait_recv()
-            copy = give(number, source, sibling, send_f.at[number, slot], recv_w.at[number, 8 + slot])
+    order = [(0, 0, 1), (0, 1, 0), (0, 3, 0), (1, 0, 1), (1, 1, 0), (1, 3, 0), (0, 2, 0), (1, 2, 0)]
+    order += [(number, dx, 1) for number in range(2) for dx in (1, 3, 2)]
+    for number, dx, dl in order:
+        slot = 2 * dx + dl
+        source = chip(4 - dx, 2 - dl, core)
+        give(number, source, sibling, send_w.at[number, slot], recv_w.at[number, slot]).wait_recv()
+        if number == 0 and dl == 1 and dx == 0:
+            onward = [(step, chip(step, 0, core)) for step in (2, 1, 3)]
+        elif number == 1 and dl == 0:
+            onward = [(dx, chip(0, 1, core))]
+        else:
+            onward = []
+        copies = [
+            give(number, source, there, send_w.at[number, 2 * step + 1], recv_w.at[number, 2 * step + 1])
+            for step, there in onward
+        ]
+        copies.append(give(number, source, sibling, send_f.at[number, slot], recv_w.at[number, 8 + slot]))
+        for copy in copies:
             copy.start()
-            sends.append(copy)
+        sends.extend(copies)
     for number in range(2):
         for dx, dl in [(0, 0)] + arrivals:
             slot = 2 * dx + dl

time: 61.6 us -> 61.7 us (level)
  no operation moved by 1% of the time
where the time goes in v4:
time: 61.7 us; the launch traced here: 61.5 us
  Pallas kernels  60.9 us (99%)
  between operations  0.64 us (1%)
    pallas_call x1, Pallas kernels, combined(): pl.pallas_call(kernel, out_shape=(jax.ShapeDtypeStruct(grad_g.shape, f32)...  54.8 us
    pallas_call x1, Pallas kernels, update(): pl.pallas_call(update_kernel, grid=(STEPS,), out_shape=[jax.ShapeDtypeStr...  6.07 us

profile of v4, /device:TPU:1, one launch (start us, length us, event | category | flops | bytes accessed | tf_op | source)
XLA Modules:
  0.0 61.5 jit_solution(16998726144426454241)
XLA Ops:
  0.6 54.8 %adasum.1 = (f32[128,1792]{1,0:T(8,128)}, f32[256,512]{1,0:T(8,128)}) custom-call(f32[128,1792]{1,0:T(8,128)} %bitcast.2, f32[256,512]{1,0:T(8,128)} %bitcast.3), custom_call_target="tpu_custom_call" | custom-call | tf_op jit(solution)/shard_map/adasum/pallas_call | solution.py:262
  55.4 6.1 %adamw.1 = (f32[128,1792]{1,0:T(8,128)}, f32[128,1792]{1,0:T(8,128)}, f32[128,1792]{1,0:T(8,128)}, f32[128,1792]{1,0:T(8,128)}, f32[256,512]{1,0:T(8,128)}, /*in...) custom-call(f32[128,1792]{1,0:T(8,128)} %get-tuple-element.10.full_g, ...), custom_call_target="tpu_custom_call" | custom-call | tf_op jit(solution)/shard_map/adamw/pallas_call | solution.py:315
